TPU v7x, 128 devices: a whole 4x4x4 slice. The times are simulated.
128 devices in a mesh: seq: 16 (over z, x), dp: 8 (over y, core).
Axes of the slice: x: 4, y: 4, z: 4, core: 2. Of those that a mesh axis runs over, the one named last changes fastest.
Arguments:
- query_input: bfloat16 [8, 8192, 2048], P('dp', 'seq'), may hold values from -300 to 300
- key_input: bfloat16 [8, 8192, 2048], P('dp', 'seq'), may hold values from -6 to 6
- value_input: bfloat16 [8, 8192, 2048], P('dp', 'seq'), may hold values from -6 to 6
- keep_blocks: int32 [8, 16], P('dp'), may hold values from 0 to 63, as said below
- dest_slots: int32 [8, 16], P('dp'), may hold values from 0 to 15, each once within a row
- proj_weights: bfloat16 [3, 2048, 2048], P(None, None, 'seq'), may hold values from -5 to 5
- cotangent: bfloat16 [8, 2048, 2048], P('dp', None, 'seq'), may hold values from -6 to 6
Outputs:
- window_out: bfloat16 [8, 8192, 2048], P('dp', 'seq')
- causal_out: bfloat16 [8, 2048, 2048], P('dp', None, 'seq')
- weight_grad: float32 [3, 2048, 2048], P(None, None, 'seq')
- row_grad: bfloat16 [8, 2048, 2048], P('dp', 'seq')
Inputs may be any that keep to these rules, and one draw needn't show every extreme that they name: `keep_blocks`: each row lists 16 distinct block numbers in increasing order, block b covering positions b * 128 to b * 128 + 127. The 4 blocks on one index of seq contribute at most 2 kept blocks, and in every document some index of seq contributes exactly 2. `dest_slots`: each row is a permutation.
All inputs are finite; a program needn't handle non-finite values.
Results may differ from a plain program's by a relative error of at most 0.015.
Values may be sent and summed in bfloat16 or wider, within the bound.
A program may use at most 192 MiB of HBM per device.

v0:
```python
import jax
import jax.numpy as jnp
from jax import lax
from jax.sharding import PartitionSpec as P

HEAD = 128
WIN = 1024
BLK = 128


def passed_along(x, axis, by):
    length = lax.axis_size(axis)
    pairs = [(i, i + by) for i in range(length) if 0 <= i + by < length]
    return lax.ppermute(x, axis, pairs)


def window_head(query_rows, key_rows, value_rows, allowed):
    score_scale = HEAD ** (-0.5)
    scores = (
        lax.dot_general(
            query_rows, key_rows, (((1,), (1,)), ((), ())), preferred_element_type=jnp.float32
        )
        * score_scale
    )
    scores = jnp.where(allowed, scores, -1e30)
    row_max = jnp.max(scores, axis=1, keepdims=True)
    weight = jnp.where(allowed, jnp.exp(scores - row_max), 0.0)
    probabilities = (weight / jnp.sum(weight, axis=1, keepdims=True)).astype(jnp.bfloat16)
    return jnp.dot(probabilities, value_rows, preferred_element_type=jnp.float32).astype(
        jnp.bfloat16
    )


def norm_rows(rows_in):
    values_f = rows_in.astype(jnp.float32)
    mean_square = jnp.mean(values_f * values_f, axis=1, keepdims=True)
    return (values_f * lax.rsqrt(mean_square + 1e-06)).astype(jnp.bfloat16)


def global_head(query_rows, key_rows, value_rows, grad_rows, positions):
    row_count = query_rows.shape[0]
    block_rows = min(512, row_count)
    block_count = row_count // block_rows
    score_scale = HEAD ** (-0.5)

    def step_block(accumulators, block_index):
        key_acc, value_acc = accumulators
        start_row = block_index * block_rows
        query_block = lax.dynamic_slice_in_dim(query_rows, start_row, block_rows, 0)
        grad_block = lax.dynamic_slice_in_dim(grad_rows, start_row, block_rows, 0)
        place_block = lax.dynamic_slice_in_dim(positions, start_row, block_rows, 0)
        causal = positions[None, :] <= place_block[:, None]
        scores = (
            lax.dot_general(
                query_block, key_rows, (((1,), (1,)), ((), ())), preferred_element_type=jnp.float32
            )
            * score_scale
        )
        scores = jnp.where(causal, scores, -1e30)
        row_max = jnp.max(scores, axis=1, keepdims=True)
        weight = jnp.where(causal, jnp.exp(scores - row_max), 0.0)
        soft_weights = weight / jnp.sum(weight, axis=1, keepdims=True)
        probabilities = soft_weights.astype(jnp.bfloat16)
        head_output = jnp.dot(probabilities, value_rows, preferred_element_type=jnp.float32).astype(
            jnp.bfloat16
        )
        d_probs = lax.dot_general(
            grad_block, value_rows, (((1,), (1,)), ((), ())), preferred_element_type=jnp.float32
        )
        value_acc = value_acc + lax.dot_general(
            probabilities, grad_block, (((0,), (0,)), ((), ())), preferred_element_type=jnp.float32
        )
        row_delta = jnp.sum(soft_weights * d_probs, axis=1, keepdims=True)
        d_scores = (soft_weights * (d_probs - row_delta) * score_scale).astype(jnp.bfloat16)
        grad_query = jnp.dot(d_scores, key_rows, preferred_element_type=jnp.float32).astype(
            jnp.bfloat16
        )
        key_acc = key_acc + lax.dot_general(
            d_scores, query_block, (((0,), (0,)), ((), ())), preferred_element_type=jnp.float32
        )
        return ((key_acc, value_acc), (head_output, grad_query))

    zero_acc = jnp.zeros(key_rows.shape, jnp.float32)
    (key_acc, value_acc), (outputs, grad_queries) = lax.scan(
        step_block, (zero_acc, zero_acc), jnp.arange(block_count)
    )
    head_width = query_rows.shape[1]
    return (
        outputs.reshape(row_count, head_width),
        grad_queries.reshape(row_count, head_width),
        key_acc.astype(jnp.bfloat16),
        value_acc.astype(jnp.bfloat16),
    )


def shards(query_input, key_input, value_input, keep_blocks, dest_slots, proj_weights, cotangent):
    query_rows = query_input[0]
    key_rows = key_input[0]
    value_rows = value_input[0]
    tok_rows, feature_width = query_rows.shape
    head_count = feature_width // HEAD
    shard_index = lax.axis_index("seq")
    seq_count = lax.axis_size("seq")
    reach_rows = WIN - 1
    depth_hops = (reach_rows + tok_rows - 1) // tok_rows
    before_keys = []
    before_values = []
    for distance in range(1, depth_hops + 1):
        need_rows = min(tok_rows, reach_rows - (distance - 1) * tok_rows)
        edge_pair = jnp.stack(
            [key_rows[tok_rows - need_rows :], value_rows[tok_rows - need_rows :]]
        )
        arrived = passed_along(edge_pair, "seq", distance)
        before_keys.insert(0, arrived[0])
        before_values.insert(0, arrived[1])
    key_ext = jnp.concatenate(before_keys + [key_rows], axis=0)
    value_ext = jnp.concatenate(before_values + [value_rows], axis=0)
    row_ids = jnp.arange(tok_rows)[:, None]
    col_ids = jnp.arange(tok_rows + reach_rows)[None, :]
    allowed = (
        (col_ids >= row_ids)
        & (col_ids <= row_ids + reach_rows)
        & (col_ids + shard_index * tok_rows >= reach_rows)
    )

    def head_window(head_index):
        column = head_index * HEAD
        return window_head(
            lax.dynamic_slice_in_dim(query_rows, column, HEAD, 1),
            lax.dynamic_slice_in_dim(key_ext, column, HEAD, 1),
            lax.dynamic_slice_in_dim(value_ext, column, HEAD, 1),
            allowed,
        )

    stacked = lax.map(head_window, jnp.arange(head_count))
    window_out = jnp.transpose(stacked, (1, 0, 2)).reshape(tok_rows, feature_width)
    keep_list = keep_blocks[0]
    slot_list = dest_slots[0]
    kept_total = keep_list.shape[0]
    per_shard = tok_rows // BLK
    most_blocks = max(1, per_shard // 2)
    order_inverse = jnp.argsort(slot_list)
    rows_total = kept_total * BLK
    compact_ids = jnp.arange(rows_total, dtype=jnp.int32)
    kept_index = order_inverse[compact_ids // BLK]
    positions = keep_list[kept_index] * BLK + compact_ids % BLK
    local_cols = proj_weights.shape[2]
    wide_weights = jnp.concatenate([proj_weights[0], proj_weights[1], proj_weights[2]], axis=1)
    own_count = rows_total // seq_count
    kept_shard = keep_list // per_shard
    first_kept = jnp.sum(kept_shard < shard_index)
    kept_count = jnp.sum(kept_shard == shard_index)
    slot_ids = jnp.arange(most_blocks)
    pick_index = jnp.minimum(first_kept + slot_ids, kept_total - 1)
    valid_mask = jnp.repeat(slot_ids < kept_count, BLK)
    local_ids = (
        (keep_list[pick_index] % per_shard * BLK)[:, None] + jnp.arange(BLK)[None, :]
    ).reshape(-1)
    packed_rows = norm_rows(jnp.where(valid_mask[:, None], window_out[local_ids], 0))
    shard_piece = lax.all_gather(packed_rows, "seq", axis=0, tiled=True)
    gathered = shard_piece
    projected = jnp.dot(shard_piece, wide_weights, preferred_element_type=jnp.float32).astype(
        jnp.bfloat16
    )
    first_of = jnp.sum(kept_shard[None, :] < kept_shard[:, None], axis=1)
    pack_start = kept_shard * (most_blocks * BLK) + (jnp.arange(kept_total) - first_of) * BLK
    packed_index = pack_start[kept_index] + compact_ids % BLK
    gathered = gathered[packed_index]
    projected = projected[packed_index]
    grad_doc = cotangent[0]
    head_index = 0
    low = head_index * HEAD
    head_result = global_head(
        projected[:, low : low + HEAD],
        projected[:, local_cols + low : local_cols + low + HEAD],
        projected[:, 2 * local_cols + low : 2 * local_cols + low + HEAD],
        grad_doc,
        positions,
    )
    outputs = head_result[0]
    grad_query = head_result[1]
    grad_key = head_result[2]
    grad_value = head_result[3]
    grad_parts = (grad_query, grad_key, grad_value)
    local_grads = jnp.stack(
        [
            lax.dot_general(
                gathered, part, (((0,), (0,)), ((), ())), preferred_element_type=jnp.float32
            )
            for part in grad_parts
        ]
    )
    weight_grad = lax.psum(local_grads.astype(jnp.bfloat16), "dp").astype(jnp.float32)
    term = jnp.zeros((own_count * lax.axis_size("seq"), feature_width), jnp.float32)
    for which_proj in range(3):
        grad_slice = grad_parts[which_proj]
        term = term + lax.dot_general(
            grad_slice,
            proj_weights[which_proj],
            (((1,), (1,)), ((), ())),
            preferred_element_type=jnp.float32,
        )
    row_grad = lax.psum_scatter(term.astype(jnp.bfloat16), "seq", scatter_dimension=0, tiled=True)
    return (window_out[None], outputs[None], weight_grad, row_grad[None])


def solution(mesh):
    return jax.shard_map(
        shards,
        mesh=mesh,
        in_specs=(
            P("dp", "seq", None),
            P("dp", "seq", None),
            P("dp", "seq", None),
            P("dp", None),
            P("dp", None),
            P(None, None, "seq"),
            P("dp", None, "seq"),
        ),
        out_specs=(
            P("dp", "seq", None),
            P("dp", None, "seq"),
            P(None, None, "seq"),
            P("dp", "seq", None),
        ),
        check_vma=False,
    )
```

profile of v0, /device:TPU:0, one launch (start us, length us, event | category | flops | bytes accessed | tf_op | source)
XLA Modules:
  0.0 815.9 jit_solution(6254746076496905836)
XLA Ops:
  9.3 3.2 copy.31
  13.1 5.2 copy.32
  18.3 10.9 %pad_maximum_fusion.1 = bf16[2,511,2048]{2,0,1:T(2,128)(2,1)} fusion(bf16[1,511,2048]{2,0,1:T(2,128)(2,1)} %copy.32, bf16[1,511,2048]{2,0,1:T(2,128)(2,1)S(1)} %copy.31), kind=kLoop, calls=%fused_computation.54 | loop fusion | flops 8372224 | bytes 8372224 | tf_op jit(solution)/shard_map/stack | solution.py:110
  29.2 7.1 collective-permute-start
  36.3 2.3 pad_maximum_fusion
  38.6 4.7 collective-permute-start.1
  46.1 79.3 %collective-permute-done = bf16[2,511,2048]{2,0,1:T(2,128)(2,1)} collective-permute-done((bf16[2,511,2048]{2,0,1:T(2,128)(2,1)}, bf16[2,511,2048]{2,0,1:T(2,128)(2,1)}, u32[]{:S(2)}, u32[]{:S(2)}) %collective-permute-start) | collective-permute-done | bytes 4186144 | tf_op jit(solution)/shard_map/ppermute | solution.py:14
  125.5 8.7 %fusion.65 = (bf16[1,511,2048]{2,0,1:T(2,128)(2,1)S(1)}, bf16[1,511,2048]{2,0,1:T(2,128)(2,1)S(1)}) fusion(bf16[2,511,2048]{2,0,1:T(2,128)(2,1)} %collective-permute-done), kind=kLoop, calls=%fused_computation.174 | loop fusion | bytes 8372224 | tf_op jit(solution)/shard_map/slice | solution.py:115
  134.1 4.7 copy_bitcast_fusion.1
  138.8 75.4 %collective-permute-done.1 = bf16[2,512,2048]{2,1,0:T(8,128)(2,1)} collective-permute-done((bf16[2,512,2048]{2,1,0:T(8,128)(2,1)}, bf16[2,512,2048]{2,1,0:T(8,128)(2,1)}, u32[]{:S(2)}, u32[]{:S(2)}) %collective-permute-start.1) | collective-permute-done | bytes 4194336 | tf_op jit(solution)/shard_map/ppermute | solution.py:14
  214.2 4.8 slice_bitcast_fusion
  219.0 31.6 %concatenate.10 = bf16[1535,2048]{1,0:T(8,128)(2,1)} concatenate(bf16[511,2048]{1,0:T(8,128)(2,1)} %get-tuple-element.281, bf16[512,2048]{1,0:T(8,128)(2,1)} %get-tuple-element.223, bf16[512,2048]{1,0:T(8,128)(2,1)S(1)} %bitcast.151), dimensions={0} | concatenate | bytes 12574720 | tf_op jit(solution)/shard_map/concatenate | solution.py:117
  250.6 33.6 %concatenate.9 = bf16[1535,2048]{1,0:T(8,128)(2,1)} concatenate(bf16[511,2048]{1,0:T(8,128)(2,1)} %get-tuple-element.282, bf16[512,2048]{1,0:T(8,128)(2,1)} %get-tuple-element.224, bf16[512,2048]{1,0:T(8,128)(2,1)} %bitcast.152), dimensions={0} | concatenate | bytes 12574720 | tf_op jit(solution)/shard_map/concatenate | solution.py:116
  284.2 110.0 %while.28 = (s32[]{:T(128)}, bf16[16,512,128]{2,1,0:T(8,128)(2,1)S(1)}, s32[16]{0:T(128)S(1)}, bf16[512,2048]{1,0:T(8,128)(2,1)}, bf16[1535,2048]{1,0:T(8,128)(2...) while((s32[]{:T(128)}, ...), condition=%wide.region_3.4_spmd.clone, body=%wide.region_0.3_spmd.clone.sunk | while | flops 419745792 | bytes 10504381 | solution.py:135
  288.8 2.3 fusion.104
  292.3 2.2 fusion.102
  295.7 2.3 fusion.104
  299.2 2.1 fusion.102
  302.6 2.3 fusion.104
  309.4 2.3 fusion.104
  313.0 2.2 fusion.102
  316.3 2.3 fusion.104
  319.9 2.1 fusion.102
  323.2 2.3 fusion.104
  330.1 2.3 fusion.104
  333.6 2.2 fusion.102
  336.9 2.3 fusion.104
  340.5 2.1 fusion.102
  343.8 2.3 fusion.104
  350.7 2.3 fusion.104
  354.2 2.2 fusion.102
  357.6 2.3 fusion.104
  361.1 2.1 fusion.102
  364.5 2.3 fusion.104
  371.3 2.3 fusion.104
  374.9 2.2 fusion.102
  378.2 2.3 fusion.104
  381.7 2.1 fusion.102
  385.1 2.3 fusion.104
  392.0 2.3 fusion.104
  404.7 4.3 compare_select_fusion.5
  409.0 5.6 select_select_fusion.1
  414.7 4.5 compare_select_fusion.12
  419.3 5.6 select_select_fusion
  425.0 4.4 compare_select_fusion.11
  429.4 5.5 fusion.51
  434.9 2.3 slice_bitcast_fusion.4
  437.2 78.3 %all-gather.2.cloned.1.call-done = bf16[4096,2048]{1,0:T(8,128)(2,1)} async-done(((bf16[256,2048]{1,0:T(8,128)(2,1)}), bf16[4096,2048]{1,0:T(8,128)(2,1)}) %all-gather.2.cloned.1.call-update) | async-done | bytes 16777232 | tf_op jit(solution)/shard_map/all_gather | solution.py:160
  515.4 13.7 %convolution_convert_fusion.2 = bf16[4096,384]{1,0:T(8,128)(2,1)} fusion(bf16[4096,2048]{1,0:T(8,128)(2,1)} %all-gather.2.cloned.1.call-done, bf16[2048,128]{1,0:T(8,128)(2,1)S(1)} %get-tuple-element.231, bf16[2048,128]{1,0:T(8,128)(2,1)} %get-tuple-element.232, bf16[2048,128]{1,0:T(8,128)(2,1)S(1)} %get-tuple-element.230), kind=kOutput, calls=%fused_computation.52 | convolution fusion | flops 6448742400 | bytes 21495808 | tf_op jit(solution)/shard_map/dot_general | solution.py:162
  529.1 11.2 %gather_fusion.2 = bf16[2048,384]{1,0:T(8,128)(2,1)} fusion(bf16[4096,384]{1,0:T(8,128)(2,1)} %convolution_convert_fusion.2, s32[2048]{0:T(1024)S(1)} %broadcast_clamp_fusion), kind=kCustom, calls=%fused_computation.2 | custom fusion | bytes 3153920 | tf_op jit(solution)/shard_map/gather | solution.py:169
  540.2 2.3 fusion.66
  542.5 58.0 %while.29 = (s32[]{:T(128)}, f32[2048,128]{1,0:T(8,128)S(1)}, f32[2048,128]{1,0:T(8,128)S(1)}, bf16[4,512,128]{2,1,0:T(8,128)(2,1)}, bf16[4,512,128]{2,1,0:T(8,1...) while((s32[]{:T(128)}, f32[2048,128]{1,0:T(8,128)S(1)}, ...), condition=%wide.region_13.14_spmd.clone, body=%wide.region_9.13_spmd.clone.sunk | while | flops 1636956672 | bytes 55361836 | solution.py:84
  600.4 9.1 %fusion.47 = f32[2048,2048]{1,0:T(8,128)} fusion(f32[2048,128]{1,0:T(8,128)S(1)} %get-tuple-element.106, bf16[3,2048,128]{2,1,0:T(8,128)(2,1)} %param.16), kind=kOutput, calls=%fused_computation.82 | convolution fusion | flops 1074003968 | bytes 18350080 | tf_op jit(solution)/shard_map/dot_general | solution.py:197
  609.5 24.5 %gather_fusion.3 = bf16[2048,2048]{1,0:T(8,128)(2,1)} fusion(bf16[4096,2048]{1,0:T(8,128)(2,1)} %all-gather.2.cloned.1.call-done, s32[2048]{0:T(1024)S(1)} %broadcast_clamp_fusion), kind=kCustom, calls=%fused_computation.3 | custom fusion | bytes 16785408 | tf_op jit(solution)/shard_map/gather | solution.py:168
  634.0 5.9 fusion.36
  640.0 2.4 fusion.35
  642.4 9.1 %fusion.62 = f32[2048,2048]{1,0:T(8,128)} fusion(bf16[2048,128]{1,0:T(8,128)(2,1)S(1)} %bitcast.156, bf16[3,2048,128]{2,1,0:T(8,128)(2,1)} %param.16), kind=kOutput, calls=%fused_computation.172 | convolution fusion | flops 1073741824 | bytes 17825792 | tf_op jit(solution)/shard_map/dot_general | solution.py:197
  651.5 2.4 fusion.37
  655.3 15.8 %add_convert_fusion = bf16[2048,2048]{1,0:T(8,128)(2,1)} fusion(f32[2048,2048]{1,0:T(8,128)} %fusion.62, f32[2048,2048]{1,0:T(8,128)} %fusion.47, f32[2048,128]{1,0:T(8,128)S(1)} %get-tuple-element.107, bf16[3,2048,128]{2,1,0:T(8,128)(2,1)} %param.16), kind=kOutput, calls=%fused_computation.51 | convolution fusion | flops 1086586880 | bytes 43515904 | tf_op jit(solution)/shard_map/dot_general | solution.py:197
  672.7 2.7 copy.29
  675.4 4.2 broadcast_in_dim_reshape.7
  679.6 39.6 %all-reduce.2.cloned.1.call-done = bf16[3,2048,128]{2,1,0:T(8,128)(2,1)} async-done(((bf16[3,2048,128]{2,1,0:T(8,128)(2,1)}), bf16[3,2048,128]{2,1,0:T(8,128)(2,1)}) %all-reduce.2.cloned.1.call-update) | async-done | bytes 1572880 | tf_op jit(solution)/shard_map/psum | solution.py:193
  719.1 3.3 convert_element_type.59
  722.4 86.5 %reduce-scatter.2.cloned.1.call-done = bf16[128,2048]{1,0:T(8,128)(2,1)} async-done(((bf16[2048,2048]{1,0:T(8,128)(2,1)}), bf16[128,2048]{1,0:T(8,128)(2,1)}) %reduce-scatter.2.cloned.1.call-update) | async-done | bytes 524304 | tf_op jit(solution)/shard_map/reduce_scatter | solution.py:203
  (165 shorter events, 107.3 us)
Async XLA Ops:
  7.2 508.2 %all-gather.2.cloned.1.call-start = ((), (), s32[]{:S(2)}) async-start(), calls=%async_computation.1 | async-start | bytes 17825792 | tf_op jit(solution)/shard_map/all_gather | solution.py:160
  9.3 3.3 copy-start.2
  18.3 18.0 %copy-start.3 = (bf16[1,512,2048]{2,1,0:T(8,128)(2,1)S(1)}, bf16[1,512,2048]{2,1,0:T(8,128)(2,1)}, u32[]{:S(2)}) copy-start(bf16[1,512,2048]{2,1,0:T(8,128)(2,1)} %param.12) | copy-start | bytes 6291460
  29.2 14.1 %copy-start = (s32[1,16]{1,0:T(1,128)S(1)}, s32[1,16]{1,0:T(1,128)}, u32[]{:S(2)}) copy-start(s32[1,16]{1,0:T(1,128)} %param.14) | copy-start | bytes 196
  29.2 96.3 %collective-permute-start = (bf16[2,511,2048]{2,0,1:T(2,128)(2,1)}, bf16[2,511,2048]{2,0,1:T(2,128)(2,1)}, u32[]{:S(2)}, u32[]{:S(2)}) collective-permute-start(bf16[2,511,2048]{2,0,1:T(2,128)(2,1)} %pad_maximum_fusion.1), channel_id=1, source_target_pairs={{0,16},{8,24},{16,32},{24,40},{32,48},{40,56},{48,64},{56,72},{64,... | collective-permute-start | bytes 12558344 | tf_op jit(solution)/shard_map/ppermute | solution.py:14
  38.6 175.6 %collective-permute-start.1 = (bf16[2,512,2048]{2,1,0:T(8,128)(2,1)}, bf16[2,512,2048]{2,1,0:T(8,128)(2,1)}, u32[]{:S(2)}, u32[]{:S(2)}) collective-permute-start(bf16[2,512,2048]{2,1,0:T(8,128)(2,1)} %pad_maximum_fusion), channel_id=1, source_target_pairs={{0,8},{8,16},{16,24},{24,32},{32,40},{40,48},{48,56},{56,64},{64,7... | collective-permute-start | bytes 12582920 | tf_op jit(solution)/shard_map/ppermute | solution.py:14
  250.6 33.6 %copy-start.4 = (bf16[16,512,128]{2,1,0:T(8,128)(2,1)S(1)}, bf16[16,512,128]{2,1,0:T(8,128)(2,1)}, u32[]{:S(2)}) copy-start(bf16[16,512,128]{2,1,0:T(8,128)(2,1)} %custom-call.10) | copy-start | bytes 6291460
  394.2 1.3 copy-start.5
  398.8 1.9 copy-start.10
  400.6 318.5 %all-reduce.2.cloned.1.call-start = ((), (), s32[]{:S(2)}) async-start(), calls=%async_computation.2 | async-start | bytes 3145728 | tf_op jit(solution)/shard_map/psum | solution.py:193
  554.1 1.2 copy-start.7
  557.1 1.0 copy-start.9
  566.5 1.2 copy-start.7
  569.5 1.0 copy-start.9
  578.9 1.2 copy-start.7
  581.9 1.0 copy-start.9
  591.3 1.2 copy-start.7
  594.3 1.0 copy-start.9
  634.0 6.0 copy-start.1
  634.0 6.0 copy-start.8
  655.3 153.7 %reduce-scatter.2.cloned.1.call-start = ((), (), s32[]{:S(2)}) async-start(), calls=%async_computation.3 | async-start | bytes 8912896 | tf_op jit(solution)/shard_map/reduce_scatter | solution.py:203
  671.2 1.6 copy-start.6
Sparse Core Ops, SparseCore 0:
  400.7 114.6 all-gather.1
  655.4 63.6 all-reduce.1
  723.1 85.7 reduce-scatter.1
where the time goes:
time: 828 us; the launch traced here: 816 us
  waiting for transfers between devices  359 us (43%)
  matrix products  165 us (20%)
  local copies, waits for them, and re-layouts  164 us (20%)
  other arithmetic  79.7 us (10%)
  loops' own time  21.7 us (3%)
  between operations  14.5 us (2%)
  starting transfers between devices  11.9 us (1%)
    ppermute x2, waiting for transfers between devices, passed_along(): return lax.ppermute(x, axis, pairs)  155 us
    reduce_scatter x1, waiting for transfers between devices, shards(): lax.psum_scatter(term.astype(jnp.bfloat16), 'seq', scatter_dimension=0, t...  86.5 us
    all_gather x1, waiting for transfers between devices, shards(): shard_piece = lax.all_gather(packed_rows, 'seq', axis=0, tiled=True)  78.3 us
    psum x1, waiting for transfers between devices, shards(): lax.psum(local_grads.astype(jnp.bfloat16), 'dp').astype(jnp.float32)  39.6 us
    dot_general x16, matrix products, window_head(): jnp.dot(probabilities, value_rows, preferred_element_type=jnp.float32)  36.5 us
    dot_general x16, matrix products, window_head(): lax.dot_general(query_rows, key_rows, (((1,), (1,)), ((), ())), preferred...  34.4 us
    dot_general x3, matrix products, shards(): lax.dot_general(grad_slice, proj_weights[which_proj], (((1,), (1,)), ((),...  34 us
    concatenate x1, local copies, waits for them, and re-layouts, shards(): key_ext = jnp.concatenate(before_keys + [key_rows], axis=0)  33.6 us
  transfers between devices with their start and end apart: 5, of which 5 were waited for; matrix products, arithmetic and copies ran while one was open for 10% of the time, Pallas kernels for 0%

commit v1 on v0

--- a/solution.py
+++ b/solution.py
@@ -157,7 +157,9 @@
         (keep_list[pick_index] % per_shard * BLK)[:, None] + jnp.arange(BLK)[None, :]
     ).reshape(-1)
     packed_rows = norm_rows(jnp.where(valid_mask[:, None], window_out[local_ids], 0))
-    shard_piece = lax.all_gather(packed_rows, "seq", axis=0, tiled=True)
+    shard_piece = jnp.concatenate(
+        lax.all_to_all(jnp.stack([packed_rows] * lax.axis_size("seq")), "seq", 0, 0), axis=0
+    )
     gathered = shard_piece
     projected = jnp.dot(shard_piece, wide_weights, preferred_element_type=jnp.float32).astype(
         jnp.bfloat16

time: 828 us -> 920 us (1.11)
  waiting for transfers between devices: 359 us -> 440 us
    all_to_all x0 -> x1, waiting for transfers between devices: none -> 214 us  [shards(): lax.all_to_all(jnp.stack([packed_rows] * lax.axis_size('seq')), 'seq', 0, 0)]
    all_gather x1 -> x0, waiting for transfers between devices: 78.3 us -> none  [shards(): shard_piece = lax.all_gather(packed_rows, 'seq', axis=0, tiled=True)]
    reduce_scatter x1, waiting for transfers between devices: 86.5 us -> 33.6 us  [shards(): lax.psum_scatter(term.astype(jnp.bfloat16), 'seq', scatter_dimension=0, t...]
  transfers between devices with their start and end apart: 5 -> 5, of which waited for: 5 -> 5; matrix products, arithmetic and copies ran while one was open for 10% -> 9% of each run, Pallas kernels for 0% -> 0%
where the time goes in v1:
time: 920 us; the launch traced here: 908 us
  waiting for transfers between devices  440 us (48%)
  local copies, waits for them, and re-layouts  170 us (18%)
  matrix products  168 us (18%)
  other arithmetic  78.9 us (9%)
  starting transfers between devices  20.7 us (2%)
  between operations  16.1 us (2%)
  loops' own time  13.8 us (2%)
    all_to_all x1, waiting for transfers between devices, shards(): lax.all_to_all(jnp.stack([packed_rows] * lax.axis_size('seq')), 'seq', 0, 0)  214 us
    ppermute x2, waiting for transfers between devices, passed_along(): return lax.ppermute(x, axis, pairs)  155 us
    psum x1, waiting for transfers between devices, shards(): lax.psum(local_grads.astype(jnp.bfloat16), 'dp').astype(jnp.float32)  37.7 us
    dot_general x16, matrix products, window_head(): jnp.dot(probabilities, value_rows, preferred_element_type=jnp.float32)  36.5 us
    dot_general x16, matrix products, window_head(): lax.dot_general(query_rows, key_rows, (((1,), (1,)), ((), ())), preferred...  34.4 us
    dot_general x3, matrix products, shards(): lax.dot_general(grad_slice, proj_weights[which_proj], (((1,), (1,)), ((),...  34.1 us
    reduce_scatter x1, waiting for transfers between devices, shards(): lax.psum_scatter(term.astype(jnp.bfloat16), 'seq', scatter_dimension=0, t...  33.6 us
    concatenate x1, local copies, waits for them, and re-layouts, shards(): key_ext = jnp.concatenate(before_keys + [key_rows], axis=0)  33.6 us
  transfers between devices with their start and end apart: 5, of which 5 were waited for; matrix products, arithmetic and copies ran while one was open for 9% of the time, Pallas kernels for 0%

profile of v1, /device:TPU:0, one launch (start us, length us, event | category | flops | bytes accessed | tf_op | source)
XLA Modules:
  0.0 908.3 jit_solution(4047306696298038531)
XLA Ops:
  10.1 3.2 copy.31
  13.9 5.2 copy.32
  19.1 10.9 %pad_maximum_fusion.1 = bf16[2,511,2048]{2,0,1:T(2,128)(2,1)} fusion(bf16[1,511,2048]{2,0,1:T(2,128)(2,1)} %copy.32, bf16[1,511,2048]{2,0,1:T(2,128)(2,1)S(1)} %copy.31), kind=kLoop, calls=%fused_computation.54 | loop fusion | flops 8372224 | bytes 8372224 | tf_op jit(solution)/shard_map/stack | solution.py:110
  30.0 7.1 collective-permute-start
  37.1 2.3 pad_maximum_fusion
  39.4 4.6 collective-permute-start.1
  46.8 79.4 %collective-permute-done = bf16[2,511,2048]{2,0,1:T(2,128)(2,1)} collective-permute-done((bf16[2,511,2048]{2,0,1:T(2,128)(2,1)}, bf16[2,511,2048]{2,0,1:T(2,128)(2,1)}, u32[]{:S(2)}, u32[]{:S(2)}) %collective-permute-start) | collective-permute-done | bytes 4186144 | tf_op jit(solution)/shard_map/ppermute | solution.py:14
  126.3 8.7 fusion.65
  134.9 4.7 copy_bitcast_fusion.1
  139.6 75.4 %collective-permute-done.1 = bf16[2,512,2048]{2,1,0:T(8,128)(2,1)} collective-permute-done((bf16[2,512,2048]{2,1,0:T(8,128)(2,1)}, bf16[2,512,2048]{2,1,0:T(8,128)(2,1)}, u32[]{:S(2)}, u32[]{:S(2)}) %collective-permute-start.1) | collective-permute-done | bytes 4194336 | tf_op jit(solution)/shard_map/ppermute | solution.py:14
  215.0 4.8 slice_bitcast_fusion
  219.8 31.6 %concatenate.10 = bf16[1535,2048]{1,0:T(8,128)(2,1)} concatenate(bf16[511,2048]{1,0:T(8,128)(2,1)} %get-tuple-element.281, bf16[512,2048]{1,0:T(8,128)(2,1)} %get-tuple-element.223, bf16[512,2048]{1,0:T(8,128)(2,1)S(1)} %bitcast.154), dimensions={0} | concatenate | bytes 12574720 | tf_op jit(solution)/shard_map/concatenate | solution.py:117
  251.4 33.6 %concatenate.9 = bf16[1535,2048]{1,0:T(8,128)(2,1)} concatenate(bf16[511,2048]{1,0:T(8,128)(2,1)} %get-tuple-element.282, bf16[512,2048]{1,0:T(8,128)(2,1)} %get-tuple-element.224, bf16[512,2048]{1,0:T(8,128)(2,1)} %bitcast.155), dimensions={0} | concatenate | bytes 12574720 | tf_op jit(solution)/shard_map/concatenate | solution.py:116
  285.0 110.0 %while.28 = (s32[]{:T(128)}, bf16[16,512,128]{2,1,0:T(8,128)(2,1)S(1)}, s32[16]{0:T(128)S(1)}, bf16[512,2048]{1,0:T(8,128)(2,1)}, bf16[1535,2048]{1,0:T(8,128)(2...) while((s32[]{:T(128)}, ...), condition=%wide.region_3.4_spmd.clone, body=%wide.region_0.3_spmd.clone.sunk | while | flops 419745792 | bytes 10504381 | solution.py:135
  289.6 2.3 fusion.104
  293.1 2.2 fusion.102
  296.5 2.3 fusion.104
  303.4 2.3 fusion.104
  310.2 2.3 fusion.104
  317.1 2.3 fusion.104
  324.0 2.3 fusion.104
  327.5 2.2 fusion.102
  330.9 2.3 fusion.104
  334.4 2.1 fusion.102
  337.7 2.3 fusion.104
  344.6 2.3 fusion.104
  348.1 2.2 fusion.102
  351.5 2.3 fusion.104
  355.0 2.1 fusion.102
  358.4 2.3 fusion.104
  365.2 2.3 fusion.104
  368.8 2.2 fusion.102
  372.1 2.3 fusion.104
  375.7 2.1 fusion.102
  379.0 2.3 fusion.104
  385.9 2.3 fusion.104
  389.4 2.2 fusion.102
  392.8 2.3 fusion.104
  400.4 6.0 stack.20
  406.4 9.0 all-to-all-start
  419.7 4.2 compare_select_fusion.5
  423.8 5.8 select_select_fusion.1
  429.6 4.3 compare_select_fusion.12
  434.1 5.8 select_select_fusion
  439.9 4.3 compare_select_fusion.11
  444.3 5.4 fusion.51
  449.6 2.3 slice_bitcast_fusion.4
  451.9 214.3 %all-to-all-done = bf16[16,256,2048]{2,1,0:T(8,128)(2,1)} async-done(((bf16[16,256,2048]{2,1,0:T(8,128)(2,1)}), bf16[16,256,2048]{2,1,0:T(8,128)(2,1)}, u32[]{:S(2)}, u32[]{:S(2)}) %all-to-all-start) | async-done | bytes 16777248 | tf_op jit(solution)/shard_map/all_to_all | solution.py:161
  666.2 24.3 %gather_fusion.3 = bf16[2048,2048]{1,0:T(8,128)(2,1)} fusion(bf16[4096,2048]{1,0:T(8,128)(2,1)} %bitcast.49, s32[2048]{0:T(1024)S(1)} %broadcast_clamp_fusion), kind=kCustom, calls=%fused_computation.3 | custom fusion | bytes 16785408 | tf_op jit(solution)/shard_map/gather | solution.py:170
  690.4 13.7 %convolution_convert_fusion.2 = bf16[4096,384]{1,0:T(8,128)(2,1)} fusion(bf16[4096,2048]{1,0:T(8,128)(2,1)} %bitcast.49, bf16[2048,128]{1,0:T(8,128)(2,1)S(1)} %get-tuple-element.231, bf16[2048,128]{1,0:T(8,128)(2,1)} %get-tuple-element.232, bf16[2048,128]{1,0:T(8,128)(2,1)S(1)} %get-tuple-element.230), kind=kOutput, calls=%fused_computation.52 | convolution fusion | flops 6448742400 | bytes 21495808 | tf_op jit(solution)/shard_map/dot_general | solution.py:164
  704.1 11.2 %gather_fusion.2 = bf16[2048,384]{1,0:T(8,128)(2,1)} fusion(bf16[4096,384]{1,0:T(8,128)(2,1)} %convolution_convert_fusion.2, s32[2048]{0:T(1024)S(1)} %broadcast_clamp_fusion), kind=kCustom, calls=%fused_computation.2 | custom fusion | bytes 3153920 | tf_op jit(solution)/shard_map/gather | solution.py:171
  715.2 2.3 fusion.66
  717.5 50.0 %while.29 = (s32[]{:T(128)}, f32[2048,128]{1,0:T(8,128)S(1)}, f32[2048,128]{1,0:T(8,128)S(1)}, bf16[4,512,128]{2,1,0:T(8,128)(2,1)}, bf16[4,512,128]{2,1,0:T(8,1...) while((s32[]{:T(128)}, f32[2048,128]{1,0:T(8,128)S(1)}, ...), condition=%wide.region_13.14_spmd.clone, body=%wide.region_9.13_spmd.clone.sunk | while | flops 1636956672 | bytes 55361836 | solution.py:84
  767.5 9.1 %fusion.47 = f32[2048,2048]{1,0:T(8,128)} fusion(f32[2048,128]{1,0:T(8,128)S(1)} %get-tuple-element.106, bf16[3,2048,128]{2,1,0:T(8,128)(2,1)} %param.16), kind=kOutput, calls=%fused_computation.82 | convolution fusion | flops 1074003968 | bytes 18350080 | tf_op jit(solution)/shard_map/dot_general | solution.py:199
  776.6 5.9 fusion.36
  782.5 5.9 fusion.35
  788.4 9.3 %fusion.62 = f32[2048,2048]{1,0:T(8,128)} fusion(bf16[2048,128]{1,0:T(8,128)(2,1)S(1)} %bitcast.159, bf16[3,2048,128]{2,1,0:T(8,128)(2,1)} %param.16), kind=kOutput, calls=%fused_computation.172 | convolution fusion | flops 1073741824 | bytes 17825792 | tf_op jit(solution)/shard_map/dot_general | solution.py:199
  797.7 2.6 fusion.37
  801.7 15.7 %add_convert_fusion = bf16[2048,2048]{1,0:T(8,128)(2,1)} fusion(f32[2048,2048]{1,0:T(8,128)} %fusion.62, f32[2048,2048]{1,0:T(8,128)} %fusion.47, f32[2048,128]{1,0:T(8,128)S(1)} %get-tuple-element.107, bf16[3,2048,128]{2,1,0:T(8,128)(2,1)} %param.16), kind=kOutput, calls=%fused_computation.51 | convolution fusion | flops 1086586880 | bytes 43515904 | tf_op jit(solution)/shard_map/dot_general | solution.py:199
  819.0 2.7 copy.29
  821.7 4.2 broadcast_in_dim_reshape.7
  825.9 37.7 %all-reduce.2.cloned.1.call-done = bf16[3,2048,128]{2,1,0:T(8,128)(2,1)} async-done(((bf16[3,2048,128]{2,1,0:T(8,128)(2,1)}), bf16[3,2048,128]{2,1,0:T(8,128)(2,1)}) %all-reduce.2.cloned.1.call-update) | async-done | bytes 1572880 | tf_op jit(solution)/shard_map/psum | solution.py:195
  863.6 3.4 convert_element_type.63
  867.0 33.6 %reduce-scatter.2.cloned.1.call-done = bf16[128,2048]{1,0:T(8,128)(2,1)} async-done(((bf16[2048,2048]{1,0:T(8,128)(2,1)}), bf16[128,2048]{1,0:T(8,128)(2,1)}) %reduce-scatter.2.cloned.1.call-update) | async-done | bytes 524304 | tf_op jit(solution)/shard_map/reduce_scatter | solution.py:205
  (168 shorter events, 110.8 us)
Async XLA Ops:
  10.1 3.3 copy-start.1
  19.1 18.0 %copy-start.2 = (bf16[1,512,2048]{2,1,0:T(8,128)(2,1)S(1)}, bf16[1,512,2048]{2,1,0:T(8,128)(2,1)}, u32[]{:S(2)}) copy-start(bf16[1,512,2048]{2,1,0:T(8,128)(2,1)} %param.12) | copy-start | bytes 6291460
  30.0 14.1 %copy-start = (s32[1,16]{1,0:T(1,128)S(1)}, s32[1,16]{1,0:T(1,128)}, u32[]{:S(2)}) copy-start(s32[1,16]{1,0:T(1,128)} %param.14) | copy-start | bytes 196
  30.0 96.3 %collective-permute-start = (bf16[2,511,2048]{2,0,1:T(2,128)(2,1)}, bf16[2,511,2048]{2,0,1:T(2,128)(2,1)}, u32[]{:S(2)}, u32[]{:S(2)}) collective-permute-start(bf16[2,511,2048]{2,0,1:T(2,128)(2,1)} %pad_maximum_fusion.1), channel_id=1, source_target_pairs={{0,16},{8,24},{16,32},{24,40},{32,48},{40,56},{48,64},{56,72},{64,... | collective-permute-start | bytes 12558344 | tf_op jit(solution)/shard_map/ppermute | solution.py:14
  39.4 175.6 %collective-permute-start.1 = (bf16[2,512,2048]{2,1,0:T(8,128)(2,1)}, bf16[2,512,2048]{2,1,0:T(8,128)(2,1)}, u32[]{:S(2)}, u32[]{:S(2)}) collective-permute-start(bf16[2,512,2048]{2,1,0:T(8,128)(2,1)} %pad_maximum_fusion), channel_id=1, source_target_pairs={{0,8},{8,16},{16,24},{24,32},{32,40},{40,48},{48,56},{56,64},{64,7... | collective-permute-start | bytes 12582920 | tf_op jit(solution)/shard_map/ppermute | solution.py:14
  251.4 33.6 %copy-start.3 = (bf16[16,512,128]{2,1,0:T(8,128)(2,1)S(1)}, bf16[16,512,128]{2,1,0:T(8,128)(2,1)}, u32[]{:S(2)}) copy-start(bf16[16,512,128]{2,1,0:T(8,128)(2,1)} %custom-call.10) | copy-start | bytes 6291460
  395.0 1.3 copy-start.4
  406.4 9.1 copy-start.9
  406.4 259.8 %all-to-all-start = ((bf16[16,256,2048]{2,1,0:T(8,128)(2,1)}), bf16[16,256,2048]{2,1,0:T(8,128)(2,1)}, u32[]{:S(2)}, u32[]{:S(2)}) async-start(bf16[16,256,2048]{2,1,0:T(8,128)(2,1)} %stack.20), calls=%async_computation | async-start | bytes 33554432 | tf_op jit(solution)/shard_map/all_to_all | solution.py:161
  415.4 448.2 %all-reduce.2.cloned.1.call-start = ((), (), s32[]{:S(2)}) async-start(), calls=%async_computation.2 | async-start | bytes 3145728 | tf_op jit(solution)/shard_map/psum | solution.py:195
  721.1 1.2 copy-start.6
  724.1 1.0 copy-start.8
  733.4 1.2 copy-start.6
  736.4 1.0 copy-start.8
  745.8 1.2 copy-start.6
  748.8 1.0 copy-start.8
  758.1 1.2 copy-start.6
  761.1 1.0 copy-start.8
  776.6 5.9 copy-start.7
  782.4 15.2 %slice-start = ((s8[8388608]{0:T(1024)(128)(4,1)}), s8[4194304]{0:T(1024)(128)(4,1)S(1)}, s32[]{:S(2)}) async-start(s8[8388608]{0:T(1024)(128)(4,1)} %bitcast.152), calls=%async_computation.4 | async-start | bytes 8388608
  788.4 9.3 %slice-start.1 = ((s8[8388608]{0:T(1024)(128)(4,1)}), s8[4194304]{0:T(1024)(128)(4,1)S(1)}, s32[]{:S(2)}) async-start(s8[8388608]{0:T(1024)(128)(4,1)} %bitcast.152), calls=%async_computation.5 | async-start | bytes 8388608
  801.6 99.0 %reduce-scatter.2.cloned.1.call-start = ((), (), s32[]{:S(2)}) async-start(), calls=%async_computation.3 | async-start | bytes 8912896 | tf_op jit(solution)/shard_map/reduce_scatter | solution.py:205
  817.4 1.6 copy-start.5
Sparse Core Ops, SparseCore 0:
  801.8 61.7 all-reduce.1
Sparse Core Ops, SparseCore 1:
  817.5 83.0 reduce-scatter.1
